TPU v7x, 32 devices: a whole 2x2x4 slice. The times are simulated.
32 devices in a mesh: grp: 2 (over y), cell: 4 (over z), snap: 2 (over x), var: 2 (over core).
Axes of the slice: x: 2, y: 2, z: 4, core: 2. Of those that a mesh axis runs over, the one named last changes fastest.
Arguments:
- q_true: bfloat16 [64, 10, 2048], P(('snap', 'var'), 'grp', 'cell'), parts along dimension 1, may hold values from -6 to 6
- coeffs: bfloat16 [64, 256], P(('snap', 'var'), 'grp'), parts along dimension 1, may hold values from -0.5 to 0.5
- basis: bfloat16 [128, 10, 2048], P(('snap', 'var'), 'grp', 'cell'), parts along dimension 1, may hold values from -6 to 6
- weights: float32 [10, 2048], P('grp', 'cell'), parts along dimension 0, may hold values from 0.0029646354 to 0.029646354
- geometry: float32 [12, 2048], P('grp', 'cell'), parts along dimension 0, may hold values from 0.2 to 1
- neighbors: int32 [12, 2048], P('grp', 'cell'), parts along dimension 0, may hold values from 0 to 767, as said below
- send_rows: int32 [4, 4, 128], P('cell', 'grp'), parts along dimension 1, may hold values from 0 to 511, as said below
- block_count: int32 [4, 2], P('cell', 'grp'), parts along dimension 1, may hold values from 2 to 4
Outputs:
- closure: float32 [64, 256], P(('snap', 'var'), 'grp'), parts along dimension 1
There are 2 independent parts, one for each index of `grp`. A program takes and returns all parts, laid end to end along the dimension named above; each array names one. Nothing has to cross between parts.
Inputs may be any that keep to these rules, and one draw needn't show every extreme that they name: neighbors[k, c] indexes a list made of the 512 cells of c's own cell shard, then the 128 cells received from the shard before, then the 128 cells received from the shard after. `send_rows`: indices local to the sending cell shard.
All inputs are finite; a program needn't handle non-finite values.
Results may differ from a plain program's by a relative error of at most 0.00091.
Values may be sent and summed in bfloat16 or wider, within the bound.
A program may use at most 64 MiB of HBM per device.

v0:
```python
import math

import jax
import jax.numpy as jnp
from jax import lax
from jax.sharding import PartitionSpec as P

BLOCK = 128


def from_behind(shard, axis, by):
    peers = lax.axis_size(axis)
    pairs = [(i, i + by) for i in range(peers) if 0 <= i + by < peers]
    return lax.ppermute(shard, axis, pairs)


def face_flux(extended, geometry, neighbors):
    cell_count = geometry.shape[1]
    var_count = extended.shape[1]
    own_cells = extended[:, :, :cell_count]
    product = extended * extended[:, 1:2, :]
    own_product = product[:, :, :cell_count]
    stacked = jnp.concatenate([extended, product], axis=1)
    running = jnp.zeros(own_cells.shape, jnp.float32)
    for face_index in range(geometry.shape[0]):
        taken = jnp.take(stacked, neighbors[face_index], axis=2)
        beside = taken[:, :var_count]
        beside_product = taken[:, var_count:]
        running = running + geometry[face_index] * (
            0.5 * (own_product + beside_product) - 0.5 * (beside - own_cells)
        )
    return running


def local(q_true, coeffs, basis, weights, geometry, neighbors, send_rows, block_count):
    snap_count, var_count, cell_count = q_true.shape
    send_lists = send_rows[0]

    def rim_rows(field):
        return (jnp.take(field, send_lists[0], axis=2), jnp.take(field, send_lists[1], axis=2))

    true_to_prev, true_to_next = rim_rows(q_true)
    whole_basis = lax.all_gather(basis, ("snap", "var"), axis=0, tiled=True)
    basis_flat = whole_basis.reshape(whole_basis.shape[0], var_count * cell_count)
    rebuilt_sum = jnp.dot(coeffs, basis_flat, preferred_element_type=jnp.float32)
    rebuilt = rebuilt_sum.astype(jnp.bfloat16).reshape(snap_count, var_count, cell_count)
    rebuilt_to_prev, rebuilt_to_next = rim_rows(rebuilt)
    true_from_prev = from_behind(true_to_next, "cell", 1)
    true_from_next = from_behind(true_to_prev, "cell", -1)
    rebuilt_from_prev = from_behind(rebuilt_to_next, "cell", 1)
    rebuilt_from_next = from_behind(rebuilt_to_prev, "cell", -1)
    true_ext = jnp.concatenate([q_true, true_from_prev, true_from_next], axis=2)
    rebuilt_ext = jnp.concatenate([rebuilt, rebuilt_from_prev, rebuilt_from_next], axis=2)
    positions = jnp.arange(cell_count, dtype=jnp.int32)
    live = (positions < block_count[0, 0] * BLOCK).astype(jnp.float32)
    group = math.gcd(snap_count, 8)
    ext_count = true_ext.shape[2]

    def snap_block(pair):
        true_part, rebuilt_part = pair
        flux_true = face_flux(true_part.astype(jnp.float32), geometry, neighbors)
        flux_rebuilt = face_flux(rebuilt_part.astype(jnp.float32), geometry, neighbors)
        return (weights * live * (flux_true - flux_rebuilt)).astype(jnp.bfloat16)

    true_groups = true_ext.reshape(snap_count // group, group, var_count, ext_count)
    rebuilt_groups = rebuilt_ext.reshape(snap_count // group, group, var_count, ext_count)
    weighted = lax.map(snap_block, (true_groups, rebuilt_groups))
    weighted_flat = weighted.reshape(snap_count, var_count * cell_count)
    contract = (((1,), (1,)), ((), ()))
    closure_part = lax.dot_general(
        weighted_flat, basis_flat, contract, preferred_element_type=jnp.float32
    )
    return lax.psum(closure_part, "cell")


def solution(mesh):
    in_specs = (
        P(("snap", "var"), "grp", "cell"),
        P(("snap", "var"), "grp"),
        P(("snap", "var"), "grp", "cell"),
        P("grp", "cell"),
        P("grp", "cell"),
        P("grp", "cell"),
        P("cell", "grp", None),
        P("cell", "grp"),
    )
    out_specs = P(("snap", "var"), "grp")
    return jax.shard_map(local, mesh=mesh, in_specs=in_specs, out_specs=out_specs, check_vma=False)
```

profile of v0, /device:TPU:0, one launch (start us, length us, event | category | flops | bytes accessed | tf_op | source)
XLA Modules:
  0.0 230.5 jit_solution(12883758674813576312)
XLA Ops:
  0.8 9.7 %all_gather.3 = bf16[128,5,512]{2,0,1:T(8,128)(2,1)S(1)} all-gather(bf16[32,5,512]{2,0,1:T(8,128)(2,1)} %param.16), channel_id=1, replica_groups=mesh['grp'=2,'cell'=4,'snap'=2,'var'=2] {'snap','var'}, dimensions={0}, use_global_device_ids=true | all-gather | bytes 819200 | tf_op jit(solution)/shard_map/all_gather | solution.py:43
  15.2 3.5 %collective-permute-start = (bf16[16,5,128]{0,1,2:T(8,128)(2,1)}, bf16[16,5,128]{0,1,2:T(8,128)(2,1)S(1)}, u32[]{:S(2)}, u32[]{:S(2)}) collective-permute-start(bf16[16,5,128]{0,1,2:T(8,128)(2,1)} %get-tuple-element.158), channel_id=1, source_target_pairs={{0,4},{4,8},{8,12},{1,5},{5,9},{9,13},{2,6},{6,10},{10,14},{3,7},{... | collective-permute-start | bytes 61448 | tf_op jit(solution)/shard_map/ppermute | solution.py:14
  21.6 4.6 %collective-permute-start.2 = (bf16[16,5,128]{0,1,2:T(8,128)(2,1)}, bf16[16,5,128]{0,1,2:T(8,128)(2,1)S(1)}, u32[]{:S(2)}, u32[]{:S(2)}) collective-permute-start(bf16[16,5,128]{0,1,2:T(8,128)(2,1)} %get-tuple-element.157), channel_id=1, source_target_pairs={{0,4},{4,8},{8,12},{1,5},{5,9},{9,13},{2,6},{6,10},{10,14},{3,7},{... | collective-permute-start | bytes 61448 | tf_op jit(solution)/shard_map/ppermute | solution.py:14
  32.1 4.0 %collective-permute-done.3 = bf16[16,5,128]{0,1,2:T(8,128)(2,1)S(1)} collective-permute-done((bf16[16,5,128]{0,1,2:T(8,128)(2,1)S(1)}, bf16[16,5,128]{0,1,2:T(8,128)(2,1)S(1)}, u32[]{:S(2)}, u32[]{:S(2)}) %collective-permute-start.3) | collective-permute-done | bytes 20512 | tf_op jit(solution)/shard_map/ppermute | solution.py:14
  36.9 181.6 %while.11 = (s32[]{:T(128)}, bf16[2,8,5,512]{3,1,2,0:T(8,128)(2,1)}, f32[5,512]{1,0:T(8,128)S(1)}, f32[6,512]{1,0:T(8,128)}, bf16[2,8,5,768]{3,1,0,2:T(8,128)(2,...) while((s32[]{:T(128)}, ...), condition=%wide.region_1.4_spmd.clone, body=%wide.region_0.3_spmd.clone.sunk | while | flops 2576898 | bytes 26133308 | solution.py:67
  52.5 2.9 %copy.164 = f32[512,8,10]{0,1,2:T(8,128)} copy(f32[512,8,10]{2,1,0:T(8,128)} %gather_fusion.11) | data formatting | bytes 327680 | tf_op jit(solution)/shard_map/while/body/eval_jaxpr/jit(_take)/gather | solution.py:26
  58.1 2.9 %copy.162 = f32[512,8,10]{0,1,2:T(8,128)} copy(f32[512,8,10]{2,1,0:T(8,128)} %gather_fusion.9) | data formatting | bytes 327680 | tf_op jit(solution)/shard_map/while/body/eval_jaxpr/jit(_take)/gather | solution.py:26
  63.6 2.9 %copy.160 = f32[512,8,10]{0,1,2:T(8,128)} copy(f32[512,8,10]{2,1,0:T(8,128)} %gather_fusion.7) | data formatting | bytes 327680 | tf_op jit(solution)/shard_map/while/body/eval_jaxpr/jit(_take)/gather | solution.py:26
  69.2 2.9 %copy.158 = f32[512,8,10]{0,1,2:T(8,128)} copy(f32[512,8,10]{2,1,0:T(8,128)} %gather_fusion.5) | data formatting | bytes 327680 | tf_op jit(solution)/shard_map/while/body/eval_jaxpr/jit(_take)/gather | solution.py:26
  74.8 2.9 %copy.156 = f32[512,8,10]{0,1,2:T(8,128)} copy(f32[512,8,10]{2,1,0:T(8,128)} %gather_fusion.3) | data formatting | bytes 327680 | tf_op jit(solution)/shard_map/while/body/eval_jaxpr/jit(_take)/gather | solution.py:26
  80.3 2.9 %copy.154 = f32[512,8,10]{0,1,2:T(8,128)} copy(f32[512,8,10]{2,1,0:T(8,128)} %gather_fusion.1) | data formatting | bytes 327680 | tf_op jit(solution)/shard_map/while/body/eval_jaxpr/jit(_take)/gather | solution.py:26
  88.2 2.9 %copy.163 = f32[512,8,10]{0,1,2:T(8,128)} copy(f32[512,8,10]{2,1,0:T(8,128)} %gather_fusion.10) | data formatting | bytes 327680 | tf_op jit(solution)/shard_map/while/body/eval_jaxpr/jit(_take)/gather | solution.py:26
  102.9 2.9 %copy.159 = f32[512,8,10]{0,1,2:T(8,128)} copy(f32[512,8,10]{2,1,0:T(8,128)} %gather_fusion.6) | data formatting | bytes 327680 | tf_op jit(solution)/shard_map/while/body/eval_jaxpr/jit(_take)/gather | solution.py:26
  117.6 2.9 %copy.155 = f32[512,8,10]{0,1,2:T(8,128)} copy(f32[512,8,10]{2,1,0:T(8,128)} %gather_fusion.2) | data formatting | bytes 327680 | tf_op jit(solution)/shard_map/while/body/eval_jaxpr/jit(_take)/gather | solution.py:26
  143.3 2.9 %copy.164 = f32[512,8,10]{0,1,2:T(8,128)} copy(f32[512,8,10]{2,1,0:T(8,128)} %gather_fusion.11) | data formatting | bytes 327680 | tf_op jit(solution)/shard_map/while/body/eval_jaxpr/jit(_take)/gather | solution.py:26
  148.9 2.9 %copy.162 = f32[512,8,10]{0,1,2:T(8,128)} copy(f32[512,8,10]{2,1,0:T(8,128)} %gather_fusion.9) | data formatting | bytes 327680 | tf_op jit(solution)/shard_map/while/body/eval_jaxpr/jit(_take)/gather | solution.py:26
  154.4 2.9 %copy.160 = f32[512,8,10]{0,1,2:T(8,128)} copy(f32[512,8,10]{2,1,0:T(8,128)} %gather_fusion.7) | data formatting | bytes 327680 | tf_op jit(solution)/shard_map/while/body/eval_jaxpr/jit(_take)/gather | solution.py:26
  160.0 2.9 %copy.158 = f32[512,8,10]{0,1,2:T(8,128)} copy(f32[512,8,10]{2,1,0:T(8,128)} %gather_fusion.5) | data formatting | bytes 327680 | tf_op jit(solution)/shard_map/while/body/eval_jaxpr/jit(_take)/gather | solution.py:26
  165.5 2.9 %copy.156 = f32[512,8,10]{0,1,2:T(8,128)} copy(f32[512,8,10]{2,1,0:T(8,128)} %gather_fusion.3) | data formatting | bytes 327680 | tf_op jit(solution)/shard_map/while/body/eval_jaxpr/jit(_take)/gather | solution.py:26
  171.1 2.9 %copy.154 = f32[512,8,10]{0,1,2:T(8,128)} copy(f32[512,8,10]{2,1,0:T(8,128)} %gather_fusion.1) | data formatting | bytes 327680 | tf_op jit(solution)/shard_map/while/body/eval_jaxpr/jit(_take)/gather | solution.py:26
  179.0 2.9 %copy.163 = f32[512,8,10]{0,1,2:T(8,128)} copy(f32[512,8,10]{2,1,0:T(8,128)} %gather_fusion.10) | data formatting | bytes 327680 | tf_op jit(solution)/shard_map/while/body/eval_jaxpr/jit(_take)/gather | solution.py:26
  193.7 2.9 %copy.159 = f32[512,8,10]{0,1,2:T(8,128)} copy(f32[512,8,10]{2,1,0:T(8,128)} %gather_fusion.6) | data formatting | bytes 327680 | tf_op jit(solution)/shard_map/while/body/eval_jaxpr/jit(_take)/gather | solution.py:26
  208.4 2.9 %copy.155 = f32[512,8,10]{0,1,2:T(8,128)} copy(f32[512,8,10]{2,1,0:T(8,128)} %gather_fusion.2) | data formatting | bytes 327680 | tf_op jit(solution)/shard_map/while/body/eval_jaxpr/jit(_take)/gather | solution.py:26
  219.8 10.7 %psum.7 = f32[16,128]{1,0:T(8,128)} all-reduce(f32[16,128]{1,0:T(8,128)S(1)} %fusion.66), channel_id=1, replica_groups=mesh['grp'=2,'cell'=4,'snap'=2,'var'=2] {'cell'}, use_global_device_ids=true, to_apply=%region_2.5 | all-reduce | flops 2048 | bytes 16384 | tf_op jit(solution)/shard_map/psum | solution.py:73
  (241 shorter events, 144.5 us)
Async XLA Ops:
  0.0 10.8 %copy-start = (bf16[16,128]{1,0:T(8,128)(2,1)S(1)}, bf16[16,128]{1,0:T(8,128)(2,1)}, u32[]{:S(2)}) copy-start(bf16[16,128]{1,0:T(8,128)(2,1)} %param.15) | copy-start | bytes 12292
  0.8 11.3 %copy-start.17 = (bf16[16,5,512]{2,0,1:T(8,128)(2,1)S(1)}, bf16[16,5,512]{2,0,1:T(8,128)(2,1)}, u32[]{:S(2)}) copy-start(bf16[16,5,512]{2,0,1:T(8,128)(2,1)} %param.14) | copy-start | bytes 245764
  10.8 4.4 %copy-start.14 = (bf16[128,5,512]{0,2,1:T(8,128)(2,1)}, bf16[128,5,512]{0,2,1:T(8,128)(2,1)S(1)}, u32[]{:S(2)}) copy-start(bf16[128,5,512]{0,2,1:T(8,128)(2,1)S(1)} %copy.124) | copy-start | bytes 1966084
  12.8 24.1 %copy-start.15 = (f32[5,512]{1,0:T(8,128)S(1)}, f32[5,512]{1,0:T(8,128)}, u32[]{:S(2)}) copy-start(f32[5,512]{1,0:T(8,128)} %param.17) | copy-start | bytes 30724
  15.2 12.9 %collective-permute-start = (bf16[16,5,128]{0,1,2:T(8,128)(2,1)}, bf16[16,5,128]{0,1,2:T(8,128)(2,1)S(1)}, u32[]{:S(2)}, u32[]{:S(2)}) collective-permute-start(bf16[16,5,128]{0,1,2:T(8,128)(2,1)} %get-tuple-element.158), channel_id=1, source_target_pairs={{0,4},{4,8},{8,12},{1,5},{5,9},{9,13},{2,6},{6,10},{10,14},{3,7},{... | collective-permute-start | bytes 61448 | tf_op jit(solution)/shard_map/ppermute | solution.py:14
  20.3 10.4 %collective-permute-start.1 = (bf16[16,5,128]{0,1,2:T(8,128)(2,1)S(1)}, bf16[16,5,128]{0,1,2:T(8,128)(2,1)S(1)}, u32[]{:S(2)}, u32[]{:S(2)}) collective-permute-start(bf16[16,5,128]{0,1,2:T(8,128)(2,1)S(1)} %get-tuple-element.160), channel_id=1, source_target_pairs={{4,0},{8,4},{12,8},{5,1},{9,5},{13,9},{6,2},{10,6},{14,10},{7,3},{... | collective-permute-start | bytes 61448 | tf_op jit(solution)/shard_map/ppermute | solution.py:14
  21.6 10.4 %collective-permute-start.2 = (bf16[16,5,128]{0,1,2:T(8,128)(2,1)}, bf16[16,5,128]{0,1,2:T(8,128)(2,1)S(1)}, u32[]{:S(2)}, u32[]{:S(2)}) collective-permute-start(bf16[16,5,128]{0,1,2:T(8,128)(2,1)} %get-tuple-element.157), channel_id=1, source_target_pairs={{0,4},{4,8},{8,12},{1,5},{5,9},{9,13},{2,6},{6,10},{10,14},{3,7},{... | collective-permute-start | bytes 61448 | tf_op jit(solution)/shard_map/ppermute | solution.py:14
  26.2 9.9 %collective-permute-start.3 = (bf16[16,5,128]{0,1,2:T(8,128)(2,1)S(1)}, bf16[16,5,128]{0,1,2:T(8,128)(2,1)S(1)}, u32[]{:S(2)}, u32[]{:S(2)}) collective-permute-start(bf16[16,5,128]{0,1,2:T(8,128)(2,1)S(1)} %get-tuple-element.159), channel_id=1, source_target_pairs={{4,0},{8,4},{12,8},{5,1},{9,5},{13,9},{6,2},{10,6},{14,10},{7,3},{... | collective-permute-start | bytes 61448 | tf_op jit(solution)/shard_map/ppermute | solution.py:14
  98.4 7.4 %copy-start.28 = (pred[512]{0:T(512)(128)(4,1)S(1)}, pred[512]{0:T(512)(128)(4,1)}, u32[]{:S(2)}) copy-start(pred[512]{0:T(512)(128)(4,1)} %compare_and_fusion.17) | copy-start | bytes 1540 | tf_op jit(solution)/shard_map/while
  105.8 7.4 %copy-start.27 = (pred[512]{0:T(512)(128)(4,1)S(1)}, pred[512]{0:T(512)(128)(4,1)}, u32[]{:S(2)}) copy-start(pred[512]{0:T(512)(128)(4,1)} %compare_and_fusion.16) | copy-start | bytes 1540 | tf_op jit(solution)/shard_map/while
  120.5 6.1 %copy-start.18 = (f32[1,512]{1,0:T(1,128)S(1)}, f32[1,512]{1,0:T(1,128)}, u32[]{:S(2)}) copy-start(f32[1,512]{1,0:T(1,128)} %get-tuple-element.261) | copy-start | bytes 6148 | tf_op jit(solution)/shard_map/while
  120.5 6.1 %copy-start.19 = (f32[1,512]{1,0:T(1,128)S(1)}, f32[1,512]{1,0:T(1,128)}, u32[]{:S(2)}) copy-start(f32[1,512]{1,0:T(1,128)} %get-tuple-element.251) | copy-start | bytes 6148 | tf_op jit(solution)/shard_map/while
  120.5 6.1 %copy-start.20 = (f32[1,512]{1,0:T(1,128)S(1)}, f32[1,512]{1,0:T(1,128)}, u32[]{:S(2)}) copy-start(f32[1,512]{1,0:T(1,128)} %get-tuple-element.253) | copy-start | bytes 6148 | tf_op jit(solution)/shard_map/while
  120.5 6.1 %copy-start.21 = (f32[1,512]{1,0:T(1,128)S(1)}, f32[1,512]{1,0:T(1,128)}, u32[]{:S(2)}) copy-start(f32[1,512]{1,0:T(1,128)} %get-tuple-element.255) | copy-start | bytes 6148 | tf_op jit(solution)/shard_map/while
  123.2 3.4 %copy-start.2 = (f32[8,5,768]{2,0,1:T(8,128)S(1)}, f32[8,5,768]{2,0,1:T(8,128)}, u32[]{:S(2)}) copy-start(f32[8,5,768]{2,0,1:T(8,128)} %copy-done.1) | copy-start | bytes 368644 | tf_op jit(solution)/shard_map/while
  123.3 3.4 %copy-start.6 = (f32[8,10,512]{2,0,1:T(8,128)S(1)}, f32[8,10,512]{2,0,1:T(8,128)}, u32[]{:S(2)}) copy-start(f32[8,10,512]{2,0,1:T(8,128)} %get-tuple-element.260) | copy-start | bytes 491524 | tf_op jit(solution)/shard_map/while
  123.3 3.4 %copy-start.7 = (f32[8,10,512]{2,0,1:T(8,128)S(1)}, f32[8,10,512]{2,0,1:T(8,128)}, u32[]{:S(2)}) copy-start(f32[8,10,512]{2,0,1:T(8,128)} %get-tuple-element.249) | copy-start | bytes 491524 | tf_op jit(solution)/shard_map/while
  123.3 3.4 %copy-start.8 = (f32[8,10,512]{2,0,1:T(8,128)S(1)}, f32[8,10,512]{2,0,1:T(8,128)}, u32[]{:S(2)}) copy-start(f32[8,10,512]{2,0,1:T(8,128)} %get-tuple-element.258) | copy-start | bytes 491524 | tf_op jit(solution)/shard_map/while
  189.2 7.4 %copy-start.28 = (pred[512]{0:T(512)(128)(4,1)S(1)}, pred[512]{0:T(512)(128)(4,1)}, u32[]{:S(2)}) copy-start(pred[512]{0:T(512)(128)(4,1)} %compare_and_fusion.17) | copy-start | bytes 1540 | tf_op jit(solution)/shard_map/while
  196.5 7.4 %copy-start.27 = (pred[512]{0:T(512)(128)(4,1)S(1)}, pred[512]{0:T(512)(128)(4,1)}, u32[]{:S(2)}) copy-start(pred[512]{0:T(512)(128)(4,1)} %compare_and_fusion.16) | copy-start | bytes 1540 | tf_op jit(solution)/shard_map/while
  211.3 6.1 %copy-start.18 = (f32[1,512]{1,0:T(1,128)S(1)}, f32[1,512]{1,0:T(1,128)}, u32[]{:S(2)}) copy-start(f32[1,512]{1,0:T(1,128)} %get-tuple-element.261) | copy-start | bytes 6148 | tf_op jit(solution)/shard_map/while
  211.3 6.1 %copy-start.19 = (f32[1,512]{1,0:T(1,128)S(1)}, f32[1,512]{1,0:T(1,128)}, u32[]{:S(2)}) copy-start(f32[1,512]{1,0:T(1,128)} %get-tuple-element.251) | copy-start | bytes 6148 | tf_op jit(solution)/shard_map/while
  211.3 6.1 %copy-start.20 = (f32[1,512]{1,0:T(1,128)S(1)}, f32[1,512]{1,0:T(1,128)}, u32[]{:S(2)}) copy-start(f32[1,512]{1,0:T(1,128)} %get-tuple-element.253) | copy-start | bytes 6148 | tf_op jit(solution)/shard_map/while
  211.3 6.1 %copy-start.21 = (f32[1,512]{1,0:T(1,128)S(1)}, f32[1,512]{1,0:T(1,128)}, u32[]{:S(2)}) copy-start(f32[1,512]{1,0:T(1,128)} %get-tuple-element.255) | copy-start | bytes 6148 | tf_op jit(solution)/shard_map/while
  (34 other events, 98.9 us)
where the time goes:
time: 232 us; the launch traced here: 230 us
  local copies, waits for them, and re-layouts  154 us (66%)
  other arithmetic  35.5 us (15%)
  blocking collectives  20.3 us (9%)
  starting transfers between devices  10.6 us (5%)
  waiting for transfers between devices  6.83 us (3%)
    gather x48, local copies, waits for them, and re-layouts, face_flux(): taken = jnp.take(stacked, neighbors[face_index], axis=2)  133 us
    select_n x24, other arithmetic, face_flux(): taken = jnp.take(stacked, neighbors[face_index], axis=2)  15.6 us
    psum x1, blocking collectives, local(): return lax.psum(closure_part, 'cell')  10.7 us
    ppermute x4, starting transfers between devices, from_behind(): return lax.ppermute(shard, axis, pairs)  10.6 us
    all_gather x1, blocking collectives, local(): whole_basis = lax.all_gather(basis, ('snap', 'var'), axis=0, tiled=True)  9.68 us
    concatenate x4, local copies, waits for them, and re-layouts, face_flux(): stacked = jnp.concatenate([extended, product], axis=1)  8.67 us
    ppermute x4, waiting for transfers between devices, from_behind(): return lax.ppermute(shard, axis, pairs)  6.83 us
    and x12, other arithmetic, face_flux(): taken = jnp.take(stacked, neighbors[face_index], axis=2)  6.67 us
  transfers between devices with their start and end apart: 4, of which 3 were waited for; matrix products, arithmetic and copies ran while one was open for 1% of the time, Pallas kernels for 0%

commit v1 on v0

v1 whole, which is shorter than its diff:
```python
import functools

import jax
import jax.numpy as jnp
from jax import lax
from jax.experimental import pallas as pl
from jax.experimental.pallas import tpu as pltpu
from jax.sharding import PartitionSpec as P

BLOCK = 128
ROWS = 32
MESH = pl.DeviceIdType.MESH
F32 = jnp.float32
BF16 = jnp.bfloat16


def dot(a, b):
    return jnp.dot(a, b, preferred_element_type=F32)


def kernel(
    fused, n_cell, q_hbm, co_hbm, basis_hbm, w_hbm, geo_hbm, nb_hbm, rows_hbm, bc_hbm, out,
    q, co, w, geo, nb, rows, bc, whole, onehot, mat_hi, mat_lo, rim, halo, field_s, diff_hi, diff_lo, parts,
    in_sem, own_sem, send_x, recv_x, send_c, recv_c, send_f, recv_f, send_h, recv_h, send_p, recv_p,
):
    var_count, snaps, cells = q.shape
    faces = geo.shape[0]
    modes = whole.shape[1]
    own_modes = basis_hbm.shape[1]
    sent = rows.shape[-1]
    ext = cells + 2 * sent
    z = lax.axis_index("cell")
    x = lax.axis_index("snap")
    c = lax.axis_index("var")
    order = [1] + [v for v in range(var_count) if v != 1]

    peers = [{"cell": lax.rem(z + d, n_cell)} for d in range(1, n_cell)]
    if fused:
        peers += [{"snap": 1 - x}, {"var": 1 - c}]
    barrier = pltpu.get_barrier_semaphore()
    for peer in peers:
        pl.semaphore_signal(barrier, inc=1, device_id=peer, device_id_type=MESH)

    loads = []
    for i, (src, dst) in enumerate(
        ((rows_hbm, rows), (q_hbm, q), (nb_hbm, nb), (geo_hbm, geo), (co_hbm, co), (w_hbm, w), (bc_hbm, bc))
    ):
        loads.append(pltpu.make_async_copy(src, dst, in_sem.at[i]))
        loads[-1].start()
    l_rows, l_q, l_nb, l_geo, l_co, l_w, l_bc = loads
    pl.semaphore_wait(barrier, len(peers))

    def mode_rows(snap, var):
        return pl.ds(pl.multiple_of((snap * 2 + var) * own_modes, own_modes), own_modes)

    own, across, to_core, forward = {}, {}, {}, {}
    if fused:
        mine = mode_rows(x, c)
        theirs = mode_rows(1 - x, c)

        def remote(src, dst, sends, recvs, v, peer):
            return pltpu.make_async_remote_copy(
                src_ref=src, dst_ref=dst, send_sem=sends.at[v], recv_sem=recvs.at[v],
                device_id=peer, device_id_type=MESH,
            )

        for v in order:
            across[v] = remote(basis_hbm.at[v], whole.at[v, mine], send_x, recv_x, v, {"snap": 1 - x})
            across[v].start()
        for v in order:
            to_core[v] = remote(basis_hbm.at[v], whole.at[v, mine], send_c, recv_c, v, {"var": 1 - c})
            to_core[v].start()
            own[v] = pltpu.make_async_copy(basis_hbm.at[v], whole.at[v, mine], own_sem.at[v])
            own[v].start()
            forward[v] = remote(whole.at[v, theirs], whole.at[v, theirs], send_f, recv_f, v, {"var": 1 - c})
    else:
        for v in order:
            own[v] = pltpu.make_async_copy(basis_hbm.at[v], whole.at[v], own_sem.at[v])
            own[v].start()

    def rim_copy(slot, side, src, dst):
        return pltpu.make_async_remote_copy(
            src_ref=src, dst_ref=dst, send_sem=send_h.at[slot, side], recv_sem=recv_h.at[slot, 1 - side],
            device_id={"cell": lax.rem(z + n_cell + 2 * side - 1, n_cell)}, device_id_type=MESH,
        )

    def rim_pair(field, v):
        if v is None:
            return [rim_copy(0, s, rim.at[0, s], halo.at[0, 1 - s]) for s in (0, 1)]
        return [rim_copy(1 + v, s, rim.at[1, s, v], halo.at[1, 1 - s, v]) for s in (0, 1)]

    def start_pair(pair):
        pl.when(z > 0)(lambda: pair[0].start())
        pl.when(z < n_cell - 1)(lambda: pair[1].start())

    @pl.when(z == 0)
    def _():
        halo[:, 0] = jnp.zeros(halo[:, 0].shape, BF16)

    @pl.when(z == n_cell - 1)
    def _():
        halo[:, 1] = jnp.zeros(halo[:, 1].shape, BF16)

    l_rows.wait()
    place = lax.broadcasted_iota(jnp.int32, (cells, sent), 0)
    for side in (0, 1):
        onehot[:, side * sent:(side + 1) * sent] = jnp.where(
            place == rows[0, side:side + 1, :], 1.0, 0.0
        ).astype(BF16)
    l_q.wait()
    true_rim = dot(q[...].reshape(var_count * snaps, cells), onehot[...]).astype(BF16)
    true_rim = true_rim.reshape(var_count, snaps, 2 * sent)
    for side in (0, 1):
        rim[0, side] = true_rim[:, :, side * sent:(side + 1) * sent]
    true_pair = rim_pair(0, None)
    start_pair(true_pair)

    l_nb.wait()
    l_geo.wait()

    def face_rows(i, carry):
        first = pl.multiple_of(i * ROWS, ROWS)
        place = lax.broadcasted_iota(jnp.int32, (ROWS, cells), 0) + first
        total = jnp.zeros((ROWS, cells), F32)
        for k in range(faces):
            total += jnp.where(nb[k:k + 1, :] == place, 0.5 * geo[k:k + 1, :], 0.0)
        high = total.astype(BF16)
        mat_hi[pl.ds(first, ROWS), :] = high
        mat_lo[pl.ds(first, ROWS), :] = (total - high.astype(F32)).astype(BF16)
        return carry

    steps = ext // ROWS
    done = 0
    for i, v in enumerate(order):
        upto = steps * (i + 1) // var_count
        lax.fori_loop(done, upto, face_rows, 0)
        done = upto
        if fused:
            across[v].wait_recv()
            forward[v].start()

    l_co.wait()
    pairs = []
    true_one = true_up = rebuilt_up = None
    for v in order:
        own[v].wait()
        if fused:
            to_core[v].wait_recv()
            forward[v].wait_recv()
        rebuilt = dot(co[...], whole[v]).astype(BF16)
        picked = dot(rebuilt, onehot[...]).astype(BF16)
        for side in (0, 1):
            rim[1, side, v] = picked[:, side * sent:(side + 1) * sent]
        pair = rim_pair(1, v)
        start_pair(pair)
        pairs.append(pair)
        e_true = q[v].astype(F32)
        e_rebuilt = rebuilt.astype(F32)
        if v == 1:
            true_up, rebuilt_up = e_true, e_rebuilt
        field_s[v] = e_true * (true_up + 1.0) - e_rebuilt * (rebuilt_up + 1.0)
        diff = e_true * (true_up - 1.0) - e_rebuilt * (rebuilt_up - 1.0)
        high = diff.astype(BF16)
        diff_hi[v, :, :cells] = high
        diff_lo[v, :, :cells] = (diff - high.astype(F32)).astype(BF16)

    lines = var_count * snaps

    def gathered(lo, hi):
        top = diff_hi[:, :, lo:hi].reshape(lines, hi - lo)
        low = diff_lo[:, :, lo:hi].reshape(lines, hi - lo)
        both = dot(jnp.concatenate([top, low], axis=0), mat_hi[lo:hi, :])
        return both[:lines] + both[lines:] + dot(top, mat_lo[lo:hi, :])

    near = gathered(0, cells)
    l_w.wait()
    l_bc.wait()
    coefficient = 0.5 * jnp.sum(geo[...], axis=0, keepdims=True)
    spot = lax.broadcasted_iota(jnp.int32, (1, cells), 1)
    live = jnp.where(spot < bc[...] * BLOCK, 1.0, 0.0)
    scale = w[...] * live

    for pair in [true_pair] + pairs:
        pl.when(z < n_cell - 1)(lambda: pair[0].wait_recv())
        pl.when(z > 0)(lambda: pair[1].wait_recv())
    for side in (0, 1):
        true_up = halo[0, side, 1].astype(F32) - 1.0
        rebuilt_up = halo[1, side, 1].astype(F32) - 1.0
        for v in range(var_count):
            diff = halo[0, side, v].astype(F32) * true_up - halo[1, side, v].astype(F32) * rebuilt_up
            high = diff.astype(BF16)
            first = cells + side * sent
            diff_hi[v, :, first:first + sent] = high
            diff_lo[v, :, first:first + sent] = (diff - high.astype(F32)).astype(BF16)
    flux = (near + gathered(cells, ext)).reshape(var_count, snaps, cells)
    total = jnp.zeros((snaps, modes), F32)
    for v in range(var_count):
        weighted = (scale[v:v + 1, :] * (coefficient * field_s[v] + flux[v])).astype(BF16)
        total += lax.dot_general(
            weighted, whole[v], (((1,), (1,)), ((), ())), preferred_element_type=F32
        )

    parts[0] = total
    sums = []
    for d in range(1, n_cell):
        copy = pltpu.make_async_remote_copy(
            src_ref=parts.at[0], dst_ref=parts.at[d], send_sem=send_p.at[d - 1], recv_sem=recv_p.at[d - 1],
            device_id={"cell": lax.rem(z + d, n_cell)}, device_id_type=MESH,
        )
        copy.start()
        sums.append(copy)
    if fused:
        for v in order:
            across[v].wait_send()
            to_core[v].wait_send()
            forward[v].wait_send()
    for pair in [true_pair] + pairs:
        pl.when(z > 0)(lambda: pair[0].wait_send())
        pl.when(z < n_cell - 1)(lambda: pair[1].wait_send())
    for copy in sums:
        copy.wait_recv()
        copy.wait_send()
    out[...] = jnp.sum(parts[...], axis=0)


def local(mesh, q_true, coeffs, basis, weights, geometry, neighbors, send_rows, block_count):
    snaps, var_count, cells = q_true.shape
    own_modes = basis.shape[0]
    faces = geometry.shape[0]
    modes = coeffs.shape[1]
    sent = send_rows.shape[-1]
    ext = cells + 2 * sent
    n_cell = mesh.shape["cell"]
    fused = mesh.shape["snap"] == 2 and mesh.shape["var"] == 2 and own_modes % 16 == 0
    if not fused:
        basis = lax.all_gather(basis, ("snap", "var"), axis=0, tiled=True)
    dma = pltpu.SemaphoreType.DMA
    vmem = pltpu.VMEM
    scratch = [
        vmem((var_count, snaps, cells), BF16),
        vmem((snaps, modes), BF16),
        vmem((var_count, cells), F32),
        vmem((faces, cells), F32),
        vmem((faces, cells), jnp.int32),
        vmem((1, 2, sent), jnp.int32),
        vmem((1, 1), jnp.int32),
        vmem((var_count, modes, cells), BF16),
        vmem((cells, 2 * sent), BF16),
        vmem((ext, cells), BF16),
        vmem((ext, cells), BF16),
        vmem((2, 2, var_count, snaps, sent), BF16),
        vmem((2, 2, var_count, snaps, sent), BF16),
        vmem((var_count, snaps, cells), F32),
        vmem((var_count, snaps, ext), BF16),
        vmem((var_count, snaps, ext), BF16),
        vmem((n_cell, snaps, modes), F32),
        dma((7,)),
        dma((var_count,)),
    ]
    scratch += [dma((var_count,)) for _ in range(6)]
    scratch += [dma((1 + var_count, 2)), dma((1 + var_count, 2)), dma((n_cell - 1,)), dma((n_cell - 1,))]
    return pl.pallas_call(
        functools.partial(kernel, fused, n_cell),
        out_shape=jax.ShapeDtypeStruct((snaps, modes), F32),
        in_specs=[pl.BlockSpec(memory_space=pl.ANY)] * 8,
        out_specs=pl.BlockSpec(memory_space=pltpu.VMEM),
        scratch_shapes=scratch,
        compiler_params=pltpu.CompilerParams(
            collective_id=0, has_side_effects=True, vmem_limit_bytes=32 * 1024 * 1024
        ),
        name="closure",
    )(
        jnp.transpose(q_true, (1, 0, 2)), coeffs, jnp.transpose(basis, (1, 0, 2)),
        weights, geometry, neighbors, send_rows, block_count,
    )


def solution(mesh):
    in_specs = (
        P(("snap", "var"), "grp", "cell"),
        P(("snap", "var"), "grp"),
        P(("snap", "var"), "grp", "cell"),
        P("grp", "cell"),
        P("grp", "cell"),
        P("grp", "cell"),
        P("cell", "grp", None),
        P("cell", "grp"),
    )
    out_specs = P(("snap", "var"), "grp")
    return jax.shard_map(
        functools.partial(local, mesh), mesh=mesh, in_specs=in_specs, out_specs=out_specs, check_vma=False
    )
```

time: 232 us -> 25 us (0.11)
  local copies, waits for them, and re-layouts: 154 us -> 5.23 us
  other arithmetic: 35.5 us -> 0 us
  blocking collectives: 20.3 us -> 0 us
  Pallas kernels: 0 us -> 18.7 us
  starting transfers between devices: 10.6 us -> 0 us
  waiting for transfers between devices: 6.83 us -> 0 us
    gather x52 -> x0, local copies, waits for them, and re-layouts: 136 us -> none  [the longest x48 133 us: face_flux(): taken = jnp.take(stacked, neighbors[face_index], axis=2)]
    pallas_call x0 -> x1, Pallas kernels: none -> 18.7 us  [local(): pl.pallas_call(functools.partial(kernel, fused, n_cell), out_shape=jax.Sh...]
    select_n x26 -> x0, other arithmetic: 16.8 us -> none  [the longest x24 15.6 us: face_flux(): taken = jnp.take(stacked, neighbors[face_index], axis=2)]
    psum x1 -> x0, blocking collectives: 10.7 us -> none  [local(): return lax.psum(closure_part, 'cell')]
    ppermute x4 -> x0, starting transfers between devices: 10.6 us -> none  [from_behind(): return lax.ppermute(shard, axis, pairs)]
    all_gather x1 -> x0, blocking collectives: 9.68 us -> none  [local(): whole_basis = lax.all_gather(basis, ('snap', 'var'), axis=0, tiled=True)]
    concatenate x4 -> x0, local copies, waits for them, and re-layouts: 8.67 us -> none  [face_flux(): stacked = jnp.concatenate([extended, product], axis=1)]
    and x13 -> x0, other arithmetic: 7.43 us -> none  [the longest x12 6.67 us: face_flux(): taken = jnp.take(stacked, neighbors[face_index], axis=2)]
  transfers between devices with their start and end apart: 4 -> 0, of which waited for: 3 -> 0; matrix products, arithmetic and copies ran while one was open for 1% -> 0% of each run, Pallas kernels for 0% -> 0%
where the time goes in v1:
time: 25 us; the launch traced here: 24.6 us
  Pallas kernels  18.7 us (75%)
  local copies, waits for them, and re-layouts  5.23 us (21%)
  between operations  0.69 us (3%)
    pallas_call x1, Pallas kernels, local(): pl.pallas_call(functools.partial(kernel, fused, n_cell), out_shape=jax.Sh...  18.7 us
    unnamed x15, local copies, waits for them, and re-layouts  5.23 us

profile of v1, /device:TPU:0, one launch (start us, length us, event | category | flops | bytes accessed | tf_op | source)
XLA Modules:
  0.0 24.6 jit_solution(9143563986469630028)
XLA Ops:
  0.0 0.0 copy-start.5
  0.7 0.0 copy-start.6
  0.7 0.0 copy-done.5
  0.7 0.7 %copy-done.6 = s32[1,2,128]{2,1,0:T(2,128)S(1)} copy-done((s32[1,2,128]{2,1,0:T(2,128)S(1)}, s32[1,2,128]{2,1,0:T(2,128)}, u32[]{:S(2)}) %copy-start.6) | copy-done | bytes 1048
  1.3 0.0 copy-start
  1.4 0.9 %copy-done = bf16[32,5,512]{2,0,1:T(8,128)(2,1)S(1)} copy-done((bf16[32,5,512]{2,0,1:T(8,128)(2,1)S(1)}, bf16[32,5,512]{2,0,1:T(8,128)(2,1)}, u32[]{:S(2)}) %copy-start) | copy-done | bytes 163864
  2.3 0.0 copy-start.1
  2.3 0.9 %copy-done.1 = bf16[16,5,512]{2,0,1:T(8,128)(2,1)S(1)} copy-done((bf16[16,5,512]{2,0,1:T(8,128)(2,1)S(1)}, bf16[16,5,512]{2,0,1:T(8,128)(2,1)}, u32[]{:S(2)}) %copy-start.1) | copy-done | bytes 81944
  3.2 0.0 copy-start.2
  3.2 0.7 %copy-done.2 = f32[5,512]{1,0:T(8,128)S(1)} copy-done((f32[5,512]{1,0:T(8,128)S(1)}, f32[5,512]{1,0:T(8,128)}, u32[]{:S(2)}) %copy-start.2) | copy-done | bytes 10264
  3.9 0.0 copy-start.3
  3.9 0.7 %copy-done.3 = f32[6,512]{1,0:T(8,128)S(1)} copy-done((f32[6,512]{1,0:T(8,128)S(1)}, f32[6,512]{1,0:T(8,128)}, u32[]{:S(2)}) %copy-start.3) | copy-done | bytes 12312
  4.6 0.0 copy-start.4
  4.6 0.7 %copy-done.4 = s32[6,512]{1,0:T(8,128)S(1)} copy-done((s32[6,512]{1,0:T(8,128)S(1)}, s32[6,512]{1,0:T(8,128)}, u32[]{:S(2)}) %copy-start.4) | copy-done | bytes 12312
  5.3 18.7 %closure.1 = f32[16,128]{1,0:T(8,128)S(1)} custom-call(bf16[5,16,512]{2,1,0:T(8,128)(2,1)S(1)} %bitcast.3, bf16[16,128]{1,0:T(8,128)(2,1)S(1)} %copy-done.5, bf16[5,32,512]{2,1,0:T(8,128)(2,1)S(1)} %bitcast.2, f32[5,512]{1,0:T(8,128)S(1)} %copy-done.2, f32[6,512]{1,0:T(8,128)S(1)} %copy-done.3, s32[6,512]{1,0:T(8,128)S(1)} %copy-done.4, ...), custom_call_target="tpu_custom_call" | custom-call | tf_op jit(solution)/shard_map/closure/pallas_call | solution.py:262
  24.0 0.6 %copy.11 = f32[16,128]{1,0:T(8,128)} copy(f32[16,128]{1,0:T(8,128)S(1)} %closure.1) | data formatting | bytes 16384
Async XLA Ops:
  0.0 0.7 %copy-start.5 = (bf16[16,128]{1,0:T(8,128)(2,1)S(1)}, bf16[16,128]{1,0:T(8,128)(2,1)}, u32[]{:S(2)}) copy-start(bf16[16,128]{1,0:T(8,128)(2,1)} %co_hbm.1) | copy-start | bytes 12292
  0.7 0.7 %copy-start.6 = (s32[1,2,128]{2,1,0:T(2,128)S(1)}, s32[1,2,128]{2,1,0:T(2,128)}, u32[]{:S(2)}) copy-start(s32[1,2,128]{2,1,0:T(2,128)} %rows_hbm.1) | copy-start | bytes 3076
  1.3 0.9 %copy-start = (bf16[32,5,512]{2,0,1:T(8,128)(2,1)S(1)}, bf16[32,5,512]{2,0,1:T(8,128)(2,1)}, u32[]{:S(2)}) copy-start(bf16[32,5,512]{2,0,1:T(8,128)(2,1)} %param.10) | copy-start | bytes 491524
  2.3 0.9 %copy-start.1 = (bf16[16,5,512]{2,0,1:T(8,128)(2,1)S(1)}, bf16[16,5,512]{2,0,1:T(8,128)(2,1)}, u32[]{:S(2)}) copy-start(bf16[16,5,512]{2,0,1:T(8,128)(2,1)} %param.8) | copy-start | bytes 245764
  3.2 0.7 %copy-start.2 = (f32[5,512]{1,0:T(8,128)S(1)}, f32[5,512]{1,0:T(8,128)}, u32[]{:S(2)}) copy-start(f32[5,512]{1,0:T(8,128)} %w_hbm.1) | copy-start | bytes 30724
  3.9 0.7 %copy-start.3 = (f32[6,512]{1,0:T(8,128)S(1)}, f32[6,512]{1,0:T(8,128)}, u32[]{:S(2)}) copy-start(f32[6,512]{1,0:T(8,128)} %geo_hbm.1) | copy-start | bytes 36868
  4.6 0.7 %copy-start.4 = (s32[6,512]{1,0:T(8,128)S(1)}, s32[6,512]{1,0:T(8,128)}, u32[]{:S(2)}) copy-start(s32[6,512]{1,0:T(8,128)} %nb_hbm.1) | copy-start | bytes 36868
